TPU v7x, 256 devices: a whole 4x4x8 slice. The times are simulated.
256 devices in a mesh: seq: 32 (over y, z), head: 4 (over x), dp: 2 (over core).
Axes of the slice: x: 4, y: 4, z: 8, core: 2. Of those that a mesh axis runs over, the one named last changes fastest.
Arguments:
- tokens: bfloat16 [65536, 2048], P(('dp', 'seq', 'head')), parts along dimension 0, may hold values from -6 to 6
- qkv_weight: bfloat16 [2048, 3, 2048], P(None, None, 'head'), may hold values from -0.125 to 0.125
- out_weight: bfloat16 [2048, 2048], P('head'), may hold values from -0.125 to 0.125
- prefix_state: float32 [32, 128, 128], P(('dp', 'head')), parts along dimension 0, may hold values from -1536 to 1536
Outputs:
- layer_out: bfloat16 [65536, 2048], P(('dp', 'seq', 'head')), parts along dimension 0
There are 2 independent parts, one for each index of `dp`. A program takes and returns all parts, laid end to end along the dimension named above; an argument that names none is the same for every part. Nothing has to cross between parts.
All inputs are finite; a program needn't handle non-finite values.
Results may differ from a plain program's by a relative error of at most 0.014.
Values may be sent and summed in bfloat16 or wider, within the bound.
A program may use at most 64 MiB of HBM per device.

v0:
```python
import jax
import jax.numpy as jnp
from jax import lax
from jax.sharding import PartitionSpec as P


def on_device(tokens, qkv_weight, out_weight, prefix_state):
    model_width = qkv_weight.shape[0]
    head_size = prefix_state.shape[1]
    group_heads = prefix_state.shape[0]
    group_width = group_heads * head_size
    flat = qkv_weight.reshape(model_width, 3 * group_width)
    projected = jnp.dot(
        lax.all_gather(tokens, "head", axis=0, tiled=True), flat, preferred_element_type=jnp.float32
    ).astype(jnp.bfloat16)
    length = projected.shape[0]
    query = projected[:, :group_width].reshape(length, group_heads, head_size)
    keys = projected[:, group_width : 2 * group_width].reshape(length, group_heads, head_size)
    values = projected[:, 2 * group_width :].reshape(length, group_heads, head_size)
    local_state = jnp.einsum("thd,the->hde", keys, values, preferred_element_type=jnp.float32)
    my_block = lax.axis_index("seq")
    piece = lax.all_gather(
        local_state[None].astype(jnp.bfloat16), "seq", axis=0, tiled=True
    ).astype(jnp.float32)
    count = piece.shape[0]
    keep = (jnp.arange(count) < my_block).astype(jnp.float32)
    carried = prefix_state + jnp.sum(piece * keep[:, None, None, None], axis=0)
    carried_low = carried.astype(jnp.bfloat16)
    block = min(512, length)
    pieces = []
    for number in range(length // block):
        lower = number * block
        upper = lower + block
        block_q = query[lower:upper]
        scores = jnp.einsum(
            "shd,thd->hst", block_q, keys[:upper], preferred_element_type=jnp.float32
        )
        causal = (lower + jnp.arange(block))[:, None] >= jnp.arange(upper)[None, :]
        weights = jnp.where(causal[None], scores, 0.0).astype(jnp.bfloat16)
        mixed = jnp.einsum(
            "hst,thd->shd", weights, values[:upper], preferred_element_type=jnp.float32
        )
        mixed = mixed + jnp.einsum(
            "shd,hde->she", block_q, carried_low, preferred_element_type=jnp.float32
        )
        factor = lax.rsqrt(jnp.mean(mixed * mixed, axis=-1, keepdims=True) + 1e-06)
        pieces.append((mixed * factor).astype(jnp.bfloat16).reshape(block, group_width))
    normed = jnp.concatenate(pieces, axis=0)
    summed = lax.psum_scatter(
        jnp.dot(normed, out_weight, preferred_element_type=jnp.float32).astype(jnp.bfloat16),
        "head",
        scatter_dimension=0,
        tiled=True,
    ).astype(jnp.float32)
    return (tokens.astype(jnp.float32) + summed).astype(jnp.bfloat16)


def solution(mesh):
    return jax.shard_map(
        on_device,
        mesh=mesh,
        in_specs=(
            P(("dp", "seq", "head"), None),
            P(None, None, "head"),
            P("head", None),
            P(("dp", "head"), None, None),
        ),
        out_specs=P(("dp", "seq", "head"), None),
        check_vma=False,
    )
```

profile of v0, /device:TPU:1, one launch (start us, length us, event | category | flops | bytes accessed | tf_op | source)
XLA Modules:
  0.0 235.1 jit_solution(14859158136180378359)
XLA Ops:
  6.5 0.7 all-gather.4.cloned.1.call-update
  7.3 8.9 %copy.22 = bf16[2048,3,512]{0,2,1:T(8,128)(2,1)} copy(bf16[2048,3,512]{2,0,1:T(8,128)(2,1)} %param.5) | data formatting | bytes 12582912 | tf_op args[1]
  16.2 47.6 %all-gather.4.cloned.1.call-done = bf16[1024,2048]{1,0:T(8,128)(2,1)} async-done(((bf16[256,2048]{1,0:T(8,128)(2,1)}), bf16[1024,2048]{1,0:T(8,128)(2,1)}) %all-gather.4.cloned.1.call-update) | async-done | bytes 4194320 | tf_op jit(solution)/shard_map/all_gather | solution.py:14
  63.8 10.1 %convolution_convert_fusion = bf16[1024,1536]{1,0:T(8,128)(2,1)S(1)} fusion(bf16[1024,2048]{1,0:T(8,128)(2,1)} %all-gather.4.cloned.1.call-done, bf16[2048,1536]{0,1:T(8,128)(2,1)} %bitcast.55), kind=kOutput, calls=%fused_computation.7 | convolution fusion | flops 6444023808 | bytes 13631488 | tf_op jit(solution)/shard_map/dot_general | solution.py:13
  73.9 1.7 copy-done.1
  75.5 1.2 slice_bitcast_fusion
  76.7 1.4 copy.38
  78.1 2.7 %convolution_convert_fusion.2 = bf16[4,128,128]{2,1,0:T(8,128)(2,1)} fusion(bf16[1024,4,128]{0,2,1:T(8,128)(2,1)} %bitcast.57, bf16[128,4,8,128]{3,2,1,0:T(8,128)(2,1)} %get-tuple-element.9), kind=kOutput, calls=%fused_computation.17 | convolution fusion | flops 134283264 | bytes 2228224 | tf_op jit(solution)/shard_map/thd,the->hde/dot_general | solution.py:20
  80.8 0.2 reduce-scatter.2.cloned.1.call-start
  81.1 0.8 iota_compare_fusion.1
  81.9 1.2 iota_compare_fusion
  83.0 3.0 %slice_bitcast_fusion.2 = (bf16[64,4,8,128]{3,2,1,0:T(8,128)(2,1)}, bf16[64,4,8,128]{3,2,1,0:T(8,128)(2,1)}, bf16[64,4,8,128]{3,2,1,0:T(8,128)(2,1)S(1)}, bf16[512,512]{1,0:T(8,128)(2,1)S(1)}) fusion(bf16[1024,1536]{1,0:T(8,128)(2,1)} %copy-done.1), kind=kLoop, calls=%fused_computation.39 | loop fusion | bytes 4194304
  86.0 1.0 copy.37
  87.0 5.4 %fusion.1 = f32[4,128,512]{2,1,0:T(8,128)} fusion(bf16[1024,4,128]{0,2,1:T(8,128)(2,1)} %bitcast.58, pred[512,1024]{1,0:T(8,128)(4,1)} %iota_compare_fusion, bf16[128,4,8,128]{3,2,1,0:T(8,128)(2,1)} %get-tuple-element.9, bf16[64,4,8,128]{3,2,1,0:T(8,128)(2,1)} %get-tuple-element.6), kind=kOutput, calls=%fused_computation.3 | convolution fusion | flops 1077936128 | bytes 4194304 | tf_op jit(solution)/shard_map/hst,thd->shd/dot_general | solution.py:40
  92.4 68.1 %all-gather.6.cloned.1.call-done = bf16[128,128,128]{2,1,0:T(8,128)(2,1)} async-done(((bf16[4,128,128]{2,1,0:T(8,128)(2,1)}), bf16[128,128,128]{2,1,0:T(8,128)(2,1)}) %all-gather.6.cloned.1.call-update) | async-done | bytes 4194320 | tf_op jit(solution)/shard_map/all_gather | solution.py:22
  160.5 3.2 %fusion = f32[4,128,128]{2,1,0:T(8,128)S(1)} fusion(bf16[32,4,128,128]{3,2,1,0:T(8,128)(2,1)} %bitcast.56, f32[32]{0:T(128)S(1)} %compare_convert_fusion), kind=kLoop, calls=%fused_computation.1 | loop fusion | flops 6225920 | bytes 4456576 | tf_op jit(solution)/shard_map/reduce_sum | solution.py:27
  163.8 1.3 fusion.26
  165.1 3.9 %multiply_reduce_fusion.1 = (f32[512,4]{0,1:T(4,128)S(1)}, f32[512,4,128]{0,2,1:T(8,128)}) fusion(f32[4,128,512]{2,1,0:T(8,128)} %fusion.26, bf16[512,4,128]{0,2,1:T(8,128)(2,1)} %bitcast.61, pred[512,512]{1,0:T(8,128)(4,1)} %iota_compare_fusion.1, bf16[64,4,8,128]{3,2,1,0:T(8,128)(2,1)} %get-tuple-element.5, bf16[64,4,8,128]{3,2,1,0:T(8,128)(2,1)S(1)} %get-tuple-element.7), kind=kOutput, calls=%fused_computation.27 | convolution fusion | flops 539752448 | bytes 3940352 | tf_op jit(solution)/shard_map/hst,thd->shd/dot_general | solution.py:40
  169.1 1.6 multiply_reduce_fusion
  170.7 1.4 multiply_convert_fusion.1
  172.1 0.1 multiply_convert_fusion
  172.2 4.3 %convolution_convert_fusion.1 = bf16[1024,2048]{1,0:T(8,128)(2,1)} fusion(bf16[512,2048]{1,0:T(8,128)(2,1)S(1)} %copy-done, bf16[512,512]{0,1:T(8,128)(2,1)S(1)} %bitcast.60, bf16[512,512]{0,1:T(8,128)(2,1)S(1)} %bitcast.59), kind=kOutput, calls=%fused_computation.8 | convolution fusion | flops 2151677952 | bytes 7340032 | tf_op jit(solution)/shard_map/dot_general | solution.py:50
  176.6 49.4 %reduce-scatter.2.cloned.1.call-done = bf16[256,2048]{1,0:T(8,128)(2,1)} async-done(((bf16[1024,2048]{1,0:T(8,128)(2,1)}), bf16[256,2048]{1,0:T(8,128)(2,1)}) %reduce-scatter.2.cloned.1.call-update) | async-done | bytes 1048592 | tf_op jit(solution)/shard_map/reduce_scatter | solution.py:49
  226.0 2.6 %add_convert_fusion = bf16[256,2048]{1,0:T(8,128)(2,1)} fusion(bf16[256,2048]{1,0:T(8,128)(2,1)} %reduce-scatter.2.cloned.1.call-done, bf16[256,2048]{1,0:T(8,128)(2,1)S(1)} %copy-done.2), kind=kLoop, calls=%fused_computation.10 | loop fusion | flops 2097152 | bytes 3145728 | tf_op jit(solution)/shard_map/convert_element_type | solution.py:55
  (18 shorter events, 0.2 us)
Async XLA Ops:
  6.5 165.7 %copy-start = (bf16[512,2048]{1,0:T(8,128)(2,1)S(1)}, bf16[512,2048]{1,0:T(8,128)(2,1)}, u32[]{:S(2)}) copy-start(bf16[512,2048]{1,0:T(8,128)(2,1)} %param.6) | copy-start | bytes 6291460
  6.5 57.3 %all-gather.4.cloned.1.call-start = ((), (), s32[]{:S(2)}) async-start(), calls=%async_computation.1 | async-start | bytes 5242880 | tf_op jit(solution)/shard_map/all_gather | solution.py:14
  7.3 153.3 %all-gather.6.cloned.1.call-start = ((), (), s32[]{:S(2)}) async-start(), calls=%async_computation.3 | async-start | bytes 4325376 | tf_op jit(solution)/shard_map/all_gather | solution.py:22
  73.9 1.7 copy-start.1
  80.8 145.1 %reduce-scatter.2.cloned.1.call-start = ((), (), s32[]{:S(2)}) async-start(), calls=%async_computation.2 | async-start | bytes 5242880 | tf_op jit(solution)/shard_map/reduce_scatter | solution.py:49
  92.4 71.3 %copy-start.4 = (f32[4,128,128]{2,1,0:T(8,128)S(1)}, f32[4,128,128]{2,1,0:T(8,128)}, u32[]{:S(2)}) copy-start(f32[4,128,128]{2,1,0:T(8,128)} %param.7) | copy-start | bytes 786436
  163.8 5.3 %copy-start.3 = (bf16[64,4,8,128]{3,2,1,0:T(8,128)(2,1)S(1)}, bf16[64,4,8,128]{3,2,1,0:T(8,128)(2,1)}, u32[]{:S(2)}) copy-start(bf16[64,4,8,128]{3,2,1,0:T(8,128)(2,1)} %get-tuple-element.6) | copy-start | bytes 1572868
  176.5 49.5 %copy-start.2 = (bf16[256,2048]{1,0:T(8,128)(2,1)S(1)}, bf16[256,2048]{1,0:T(8,128)(2,1)}, u32[]{:S(2)}) copy-start(bf16[256,2048]{1,0:T(8,128)(2,1)} %param.4) | copy-start | bytes 3145732
Sparse Core Ops, SparseCore 0:
  9.2 54.5 all-gather.3
  81.0 79.5 all-gather.5
  176.7 49.2 reduce-scatter.1
where the time goes:
time: 236 us; the launch traced here: 235 us
  waiting for transfers between devices  166 us (70%)
  matrix products  29.4 us (12%)
  local copies, waits for them, and re-layouts  17.1 us (7%)
  between operations  13.2 us (6%)
  other arithmetic  9.26 us (4%)
    all_gather x1, waiting for transfers between devices, on_device(): lax.all_gather(local_state[None].astype(jnp.bfloat16), 'seq', axis=0, til...  68.1 us
    reduce_scatter x1, waiting for transfers between devices, on_device(): lax.psum_scatter(jnp.dot(normed, out_weight, preferred_element_type=jnp.f...  49.4 us
    all_gather x1, waiting for transfers between devices, on_device(): lax.all_gather(tokens, 'head', axis=0, tiled=True)  47.6 us
    unnamed x13, local copies, waits for them, and re-layouts  14.7 us
    dot_general x1, matrix products, on_device(): jnp.dot(lax.all_gather(tokens, 'head', axis=0, tiled=True), flat, preferr...  10.1 us
    dot_general x2, matrix products, on_device(): jnp.einsum('hst,thd->shd', weights, values[:upper], preferred_element_typ...  9.34 us
  transfers between devices with their start and end apart: 3, of which 3 were waited for; matrix products, arithmetic and copies ran while one was open for 9% of the time, Pallas kernels for 0%

commit v1 on v0

--- a/solution.py
+++ b/solution.py
@@ -19,8 +19,11 @@
     values = projected[:, 2 * group_width :].reshape(length, group_heads, head_size)
     local_state = jnp.einsum("thd,the->hde", keys, values, preferred_element_type=jnp.float32)
     my_block = lax.axis_index("seq")
-    piece = lax.all_gather(
-        local_state[None].astype(jnp.bfloat16), "seq", axis=0, tiled=True
+    piece = jnp.concatenate(
+        lax.all_to_all(
+            jnp.stack([local_state[None].astype(jnp.bfloat16)] * lax.axis_size("seq")), "seq", 0, 0
+        ),
+        axis=0,
     ).astype(jnp.float32)
     count = piece.shape[0]
     keep = (jnp.arange(count) < my_block).astype(jnp.float32)

time: 236 us -> 260 us (1.10)
  waiting for transfers between devices: 166 us -> 180 us
  starting transfers between devices: 0.26 us -> 9.93 us
  local copies, waits for them, and re-layouts: 17.1 us -> 20.1 us
    all_to_all x0 -> x1, waiting for transfers between devices: none -> 82 us  [on_device(): lax.all_to_all(jnp.stack([local_state[None].astype(jnp.bfloat16)] * lax.a...]
    all_gather x1 -> x0, waiting for transfers between devices: 68.1 us -> none  [on_device(): lax.all_gather(local_state[None].astype(jnp.bfloat16), 'seq', axis=0, til...]
    all_to_all x0 -> x1, starting transfers between devices: none -> 9.7 us  [on_device(): lax.all_to_all(jnp.stack([local_state[None].astype(jnp.bfloat16)] * lax.a...]
    another operation x0 -> x1, local copies, waits for them, and re-layouts: none -> 3.03 us  [on_device(): jnp.stack([local_state[None].astype(jnp.bfloat16)] * lax.axis_size('seq'))]
    unnamed x13 -> x19, local copies, waits for them, and re-layouts: 14.7 us -> 14.8 us
  transfers between devices with their start and end apart: 3 -> 3, of which waited for: 3 -> 3; matrix products, arithmetic and copies ran while one was open for 9% -> 7% of each run, Pallas kernels for 0% -> 0%
where the time goes in v1:
time: 260 us
  waiting for transfers between devices  180 us (69%)
  matrix products  27.5 us (11%)
  local copies, waits for them, and re-layouts  20.1 us (8%)
  between operations  13.5 us (5%)
  starting transfers between devices  9.93 us (4%)
  other arithmetic  8.72 us (3%)
    all_to_all x1, waiting for transfers between devices, on_device(): lax.all_to_all(jnp.stack([local_state[None].astype(jnp.bfloat16)] * lax.a...  82 us
    reduce_scatter x1, waiting for transfers between devices, on_device(): lax.psum_scatter(jnp.dot(normed, out_weight, preferred_element_type=jnp.f...  49.8 us
    all_gather x1, waiting for transfers between devices, on_device(): lax.all_gather(tokens, 'head', axis=0, tiled=True)  47.6 us
    unnamed x19, local copies, waits for them, and re-layouts  14.8 us
    dot_general x1, matrix products, on_device(): jnp.dot(lax.all_gather(tokens, 'head', axis=0, tiled=True), flat, preferr...  10.1 us
    all_to_all x1, starting transfers between devices, on_device(): lax.all_to_all(jnp.stack([local_state[None].astype(jnp.bfloat16)] * lax.a...  9.7 us
    dot_general x2, matrix products, on_device(): jnp.einsum('hst,thd->shd', weights, values[:upper], preferred_element_typ...  9.34 us
  transfers between devices with their start and end apart: 3, of which 3 were waited for; matrix products, arithmetic and copies ran while one was open for 7% of the time, Pallas kernels for 0%

profile of v1, /device:TPU:1, one launch (start us, length us, event | category | flops | bytes accessed | tf_op | source)
XLA Modules:
  0.0 259.9 jit_solution(15386912755986424045)
XLA Ops:
  6.5 0.7 all-gather.2.cloned.1.call-update
  7.3 8.9 %copy.35 = bf16[2048,3,512]{0,2,1:T(8,128)(2,1)} copy(bf16[2048,3,512]{2,0,1:T(8,128)(2,1)} %param.5) | data formatting | bytes 12582912 | tf_op args[1]
  16.2 47.6 %all-gather.2.cloned.1.call-done = bf16[1024,2048]{1,0:T(8,128)(2,1)} async-done(((bf16[256,2048]{1,0:T(8,128)(2,1)}), bf16[1024,2048]{1,0:T(8,128)(2,1)}) %all-gather.2.cloned.1.call-update) | async-done | bytes 4194320 | tf_op jit(solution)/shard_map/all_gather | solution.py:14
  63.8 10.1 %convolution_convert_fusion = bf16[1024,1536]{1,0:T(8,128)(2,1)S(1)} fusion(bf16[1024,2048]{1,0:T(8,128)(2,1)} %all-gather.2.cloned.1.call-done, bf16[2048,1536]{0,1:T(8,128)(2,1)} %bitcast.56), kind=kOutput, calls=%fused_computation.7 | convolution fusion | flops 6444023808 | bytes 13631488 | tf_op jit(solution)/shard_map/dot_general | solution.py:13
  73.9 1.7 copy-done.1
  75.6 1.2 slice_bitcast_fusion
  76.8 1.3 copy.51
  78.1 2.1 convolution_convert_fusion.2
  80.2 3.0 %stack.2 = bf16[32,1,4,128,128]{4,3,2,1,0:T(8,128)(2,1)} broadcast(bf16[4,128,128]{2,1,0:T(8,128)(2,1)S(1)} %convolution_convert_fusion.2), dimensions={2,3,4} | broadcast | bytes 4325376 | tf_op jit(solution)/shard_map/stack | solution.py:24
  83.2 9.7 %all-to-all-start = ((bf16[32,1,4,128,128]{4,3,2,1,0:T(8,128)(2,1)}), bf16[32,1,4,128,128]{4,3,2,1,0:T(8,128)(2,1)}, u32[]{:S(2)}, u32[]{:S(2)}) async-start(bf16[32,1,4,128,128]{4,3,2,1,0:T(8,128)(2,1)} %stack.2), calls=%async_computation | async-start | bytes 8388608 | tf_op jit(solution)/shard_map/all_to_all | solution.py:23
  92.9 0.2 reduce-scatter.2.cloned.1.call-start
  93.3 1.2 iota_compare_fusion
  94.4 2.9 %slice_bitcast_fusion.2 = (bf16[64,4,8,128]{3,2,1,0:T(8,128)(2,1)}, bf16[64,4,8,128]{3,2,1,0:T(8,128)(2,1)S(1)}, bf16[64,4,8,128]{3,2,1,0:T(8,128)(2,1)}, bf16[512,512]{1,0:T(8,128)(2,1)S(1)}) fusion(bf16[1024,1536]{1,0:T(8,128)(2,1)} %copy-done.1), kind=kLoop, calls=%fused_computation.39 | loop fusion | bytes 4194304
  97.4 1.0 copy.50
  98.4 5.3 %fusion.1 = f32[4,128,512]{2,1,0:T(8,128)} fusion(bf16[1024,4,128]{0,2,1:T(8,128)(2,1)} %bitcast.58, pred[512,1024]{1,0:T(8,128)(4,1)} %iota_compare_fusion, bf16[128,4,8,128]{3,2,1,0:T(8,128)(2,1)} %get-tuple-element.9, bf16[64,4,8,128]{3,2,1,0:T(8,128)(2,1)S(1)} %get-tuple-element.6), kind=kOutput, calls=%fused_computation.3 | convolution fusion | flops 1077936128 | bytes 4194304 | tf_op jit(solution)/shard_map/hst,thd->shd/dot_general | solution.py:43
  103.7 82.0 %all-to-all-done = bf16[32,1,4,128,128]{4,3,2,1,0:T(8,128)(2,1)} async-done(((bf16[32,1,4,128,128]{4,3,2,1,0:T(8,128)(2,1)}), bf16[32,1,4,128,128]{4,3,2,1,0:T(8,128)(2,1)}, u32[]{:S(2)}, u32[]{:S(2)}) %all-to-all-start) | async-done | bytes 4194336 | tf_op jit(solution)/shard_map/all_to_all | solution.py:23
  185.7 3.4 %fusion = f32[4,128,128]{2,1,0:T(8,128)S(1)} fusion(bf16[32,1,4,128,128]{4,3,2,1,0:T(8,128)(2,1)} %all-to-all-done, f32[32]{0:T(128)S(1)} %compare_convert_fusion), kind=kLoop, calls=%fused_computation.1 | loop fusion | flops 6225920 | bytes 4456576 | tf_op jit(solution)/shard_map/reduce_sum | solution.py:30
  189.1 0.4 multiply_reduce_fusion
  189.5 1.3 fusion.26
  190.8 4.0 %multiply_reduce_fusion.1 = (f32[512,4]{0,1:T(4,128)S(1)}, f32[512,4,128]{0,2,1:T(8,128)}) fusion(f32[4,128,512]{2,1,0:T(8,128)} %fusion.26, bf16[512,4,128]{0,2,1:T(8,128)(2,1)} %bitcast.61, pred[512,512]{1,0:T(8,128)(4,1)S(1)} %iota_compare_fusion.1, bf16[64,4,8,128]{3,2,1,0:T(8,128)(2,1)} %get-tuple-element.5, bf16[64,4,8,128]{3,2,1,0:T(8,128)(2,1)} %get-tuple-element.7), kind=kOutput, calls=%fused_computation.27 | convolution fusion | flops 539752448 | bytes 3940352 | tf_op jit(solution)/shard_map/hst,thd->shd/dot_general | solution.py:43
  195.0 1.4 multiply_convert_fusion.1
  196.4 4.3 %convolution_convert_fusion.1 = bf16[1024,2048]{1,0:T(8,128)(2,1)} fusion(bf16[512,2048]{1,0:T(8,128)(2,1)S(1)} %copy-done, bf16[512,512]{0,1:T(8,128)(2,1)S(1)} %bitcast.59, bf16[512,512]{0,1:T(8,128)(2,1)S(1)} %bitcast.60), kind=kOutput, calls=%fused_computation.8 | convolution fusion | flops 2151677952 | bytes 7340032 | tf_op jit(solution)/shard_map/dot_general | solution.py:53
  200.7 49.8 %reduce-scatter.2.cloned.1.call-done = bf16[256,2048]{1,0:T(8,128)(2,1)} async-done(((bf16[1024,2048]{1,0:T(8,128)(2,1)}), bf16[256,2048]{1,0:T(8,128)(2,1)}) %reduce-scatter.2.cloned.1.call-update) | async-done | bytes 1048592 | tf_op jit(solution)/shard_map/reduce_scatter | solution.py:52
  250.5 2.6 add_convert_fusion
  (24 shorter events, 0.3 us)
Async XLA Ops:
  6.5 189.8 %copy-start = (bf16[512,2048]{1,0:T(8,128)(2,1)S(1)}, bf16[512,2048]{1,0:T(8,128)(2,1)}, u32[]{:S(2)}) copy-start(bf16[512,2048]{1,0:T(8,128)(2,1)} %param.6) | copy-start | bytes 6291460
  6.5 57.3 %all-gather.2.cloned.1.call-start = ((), (), s32[]{:S(2)}) async-start(), calls=%async_computation.2 | async-start | bytes 5242880 | tf_op jit(solution)/shard_map/all_gather | solution.py:14
  73.9 1.7 copy-start.1
  83.2 102.5 %all-to-all-start = ((bf16[32,1,4,128,128]{4,3,2,1,0:T(8,128)(2,1)}), bf16[32,1,4,128,128]{4,3,2,1,0:T(8,128)(2,1)}, u32[]{:S(2)}, u32[]{:S(2)}) async-start(bf16[32,1,4,128,128]{4,3,2,1,0:T(8,128)(2,1)} %stack.2), calls=%async_computation | async-start | bytes 8388608 | tf_op jit(solution)/shard_map/all_to_all | solution.py:23
  92.9 157.6 %reduce-scatter.2.cloned.1.call-start = ((), (), s32[]{:S(2)}) async-start(), calls=%async_computation.3 | async-start | bytes 5242880 | tf_op jit(solution)/shard_map/reduce_scatter | solution.py:52
  97.4 6.3 %copy-start.4 = (bf16[64,4,8,128]{3,2,1,0:T(8,128)(2,1)}, bf16[64,4,8,128]{3,2,1,0:T(8,128)(2,1)S(1)}, u32[]{:S(2)}) copy-start(bf16[64,4,8,128]{3,2,1,0:T(8,128)(2,1)S(1)} %get-tuple-element.6) | copy-start | bytes 1572868
  103.7 85.4 %copy-start.7 = (f32[4,128,128]{2,1,0:T(8,128)S(1)}, f32[4,128,128]{2,1,0:T(8,128)}, u32[]{:S(2)}) copy-start(f32[4,128,128]{2,1,0:T(8,128)} %param.7) | copy-start | bytes 786436
  185.7 3.4 %copy-start.5 = (bf16[64,4,8,128]{3,2,1,0:T(8,128)(2,1)S(1)}, bf16[64,4,8,128]{3,2,1,0:T(8,128)(2,1)}, u32[]{:S(2)}) copy-start(bf16[64,4,8,128]{3,2,1,0:T(8,128)(2,1)} %copy-done.4) | copy-start | bytes 1572868
  185.7 3.4 %copy-start.6 = (f32[4,128,512]{2,1,0:T(8,128)S(1)}, f32[4,128,512]{2,1,0:T(8,128)}, u32[]{:S(2)}) copy-start(f32[4,128,512]{2,1,0:T(8,128)} %fusion.1) | copy-start | bytes 3145732
  185.7 3.8 %copy-start.3 = (bf16[64,4,8,128]{3,2,1,0:T(8,128)(2,1)S(1)}, bf16[64,4,8,128]{3,2,1,0:T(8,128)(2,1)}, u32[]{:S(2)}) copy-start(bf16[64,4,8,128]{3,2,1,0:T(8,128)(2,1)} %get-tuple-element.7) | copy-start | bytes 1572868
  200.7 49.8 %copy-start.2 = (bf16[256,2048]{1,0:T(8,128)(2,1)S(1)}, bf16[256,2048]{1,0:T(8,128)(2,1)}, u32[]{:S(2)}) copy-start(bf16[256,2048]{1,0:T(8,128)(2,1)} %param.4) | copy-start | bytes 3145732
Sparse Core Ops, SparseCore 0:
  9.2 54.5 all-gather.1
  200.8 49.5 reduce-scatter.1
